TPU v7x, 512 devices: a whole 4x8x8 slice. The times are simulated.
512 devices in a mesh: dp: 16 (over y_hi, x, core), seq: 32 (over z, y_lo).
Axes of the slice: x: 4, y: 8 (y_hi: 2, y_lo: 4; y = y_hi * 4 + y_lo), z: 8, core: 2. Of those that a mesh axis runs over, the one named last changes fastest.
Arguments:
- pre_gate: bfloat16 [16, 4096, 2048], P('dp', 'seq'), may hold values from -6 to 6
- post_gate: bfloat16 [16, 4096, 2048], P('dp', 'seq'), may hold values from -6 to 6
- values: bfloat16 [16, 4096, 2048], P('dp', 'seq'), may hold values from -6 to 6
- cotangent: bfloat16 [16, 4096, 2048], P('dp', 'seq'), may hold values from -6 to 6
- filters: bfloat16 [1024, 16], P(('dp', 'seq')), may hold values from -0.1875 to 0.1875
Outputs:
- output: bfloat16 [16, 4096, 2048], P('dp', 'seq')
- grad_pre: bfloat16 [16, 4096, 2048], P('dp', 'seq')
- grad_post: bfloat16 [16, 4096, 2048], P('dp', 'seq')
- grad_values: bfloat16 [16, 4096, 2048], P('dp', 'seq')
- grad_filters: float32 [1024, 16], P(('dp', 'seq'))
All inputs are finite; a program needn't handle non-finite values.
Results may differ from a plain program's by a relative error of at most 0.005.
Values may be sent and summed in bfloat16 or wider, within the bound.
A program may use at most 128 MiB of HBM per device.

v0:
```python
import jax
import jax.numpy as jnp
import numpy as np
from jax import lax
from jax.sharding import PartitionSpec as P

K = 1024


def shifted(value, axis, steps):
    count = lax.axis_size(axis)
    first, last = (max(0, -steps), min(count, count - steps))
    return lax.ppermute(value, axis, [(source, source + steps) for source in range(first, last)])


def tile_index(lag_blocks, shard_len):
    offsets = np.arange(lag_blocks)[:, None, None] * shard_len
    rows_idx = np.arange(shard_len)[None, :, None]
    cols_idx = np.arange(shard_len)[None, None, :]
    return (offsets + rows_idx - cols_idx + shard_len).astype(np.int32)


def build_tiles(all_taps, lag_blocks, shard_len):
    tap_count = all_taps.shape[0]
    needed = (lag_blocks + 1) * shard_len
    trailing = max(needed - shard_len - tap_count, 0)
    padded = jnp.concatenate(
        [
            jnp.zeros((shard_len, all_taps.shape[1]), all_taps.dtype),
            all_taps,
            jnp.zeros((trailing, all_taps.shape[1]), all_taps.dtype),
        ],
        axis=0,
    )
    columns = padded.T
    return columns[:, tile_index(lag_blocks, shard_len)]


def earlier_relay(piece_in, history_len):

    def earlier_advance(moving, unused):
        arrived = shifted(moving, "seq", 1)
        return (arrived, arrived)

    unused_last, stacked = lax.scan(earlier_advance, piece_in, None, length=history_len)
    return jnp.concatenate([piece_in[None], stacked], axis=0)


def later_relay(piece_in, history_len):

    def later_advance(moving, unused):
        arrived = shifted(moving, "seq", -1)
        return (arrived, arrived)

    unused_last, stacked = lax.scan(later_advance, piece_in, None, length=history_len)
    return jnp.concatenate([piece_in[None], stacked], axis=0)


def lag_window(gated_rows, history, local_groups, group_width, lag_count):
    row_count = gated_rows.shape[0]
    span_len = history.shape[0]
    front_zero = jnp.zeros((row_count, history.shape[1]), history.dtype)
    widened = jnp.concatenate([front_zero, history], axis=0)
    gated_grp = gated_rows.reshape(row_count, local_groups, group_width).transpose(1, 0, 2)
    hist_grp = widened.reshape(span_len + row_count, local_groups, group_width).transpose(1, 0, 2)

    def one_group(pair_in):
        gated_one, hist_one = pair_in
        product = lax.dot_general(
            gated_one, hist_one, (((1,), (1,)), ((), ())), preferred_element_type=jnp.float32
        )
        padded = jnp.pad(product, ((0, 0), (0, row_count)))
        flat_line = jnp.concatenate(
            [padded.reshape(-1), jnp.zeros((row_count,), jnp.float32)], axis=0
        )
        skewed = flat_line.reshape(row_count, span_len + 2 * row_count + 1)
        diag_sums = jnp.sum(skewed, axis=0)
        return jnp.flip(diag_sums[1 : span_len + 1], axis=0)[:lag_count]

    return lax.map(one_group, (gated_grp, hist_grp))


def shards(pre_gate, post_gate, values, cotangent, filters):
    shard_len = pre_gate.shape[1]
    channels = pre_gate.shape[2]
    groups = filters.shape[1]
    group_size = channels // groups
    seq_count = lax.axis_size("seq")
    all_taps = lax.all_gather(filters, ("dp", "seq"), axis=0, tiled=True)
    mixed_in = (pre_gate[0].astype(jnp.float32) * values[0]).astype(jnp.bfloat16)
    gated = (cotangent[0].astype(jnp.float32) * post_gate[0]).astype(jnp.bfloat16)
    history_len = min(-(-K // shard_len), seq_count - 1)
    lag_blocks = history_len + 1
    mixed_ext = earlier_relay(mixed_in, history_len)
    gated_ext = later_relay(gated, history_len)
    mixed_four = mixed_ext.reshape(lag_blocks, shard_len, groups, group_size)
    gated_four = gated_ext.reshape(lag_blocks, shard_len, groups, group_size)
    tiles = build_tiles(all_taps, lag_blocks, shard_len)
    convolved = jnp.einsum(
        "gmij,mjgc->igc", tiles, mixed_four, preferred_element_type=jnp.float32
    ).reshape(shard_len, channels)
    carried = jnp.einsum(
        "gmji,mjgc->igc", tiles, gated_four, preferred_element_type=jnp.float32
    ).reshape(shard_len, channels)
    hist_len = lag_blocks * shard_len
    lag_count = min(K, hist_len)
    history = jnp.flip(mixed_ext, axis=0).reshape(hist_len, channels)
    lag_local = lag_window(gated, history, groups, group_size, lag_count)
    partial_grads = lag_local.T
    output = (post_gate[0].astype(jnp.float32) * convolved).astype(jnp.bfloat16)
    grad_post = (cotangent[0].astype(jnp.float32) * convolved).astype(jnp.bfloat16)
    grad_pre = (carried * values[0]).astype(jnp.bfloat16)
    grad_values = (carried * pre_gate[0]).astype(jnp.bfloat16)
    owned = lax.psum_scatter(partial_grads, ("dp", "seq"), scatter_dimension=0, tiled=True)
    total_tokens = lax.axis_size("dp") * shard_len * seq_count * group_size
    grad_filters = owned / float(total_tokens**0.5)
    return (output[None], grad_pre[None], grad_post[None], grad_values[None], grad_filters)


def solution(mesh):
    return jax.shard_map(
        shards,
        mesh=mesh,
        in_specs=(
            P("dp", "seq", None),
            P("dp", "seq", None),
            P("dp", "seq", None),
            P("dp", "seq", None),
            P(("dp", "seq"), None),
        ),
        out_specs=(
            P("dp", "seq", None),
            P("dp", "seq", None),
            P("dp", "seq", None),
            P("dp", "seq", None),
            P(("dp", "seq"), None),
        ),
        check_vma=False,
    )
```

profile of v0, /device:TPU:24, one launch (start us, length us, event | category | flops | bytes accessed | tf_op | source)
XLA Modules:
  0.0 2391.0 jit_solution(9912820649971849793)
XLA Ops:
  7.2 1.3 fusion.20
  9.6 1234.1 %all-gather = bf16[512,2,16]{2,1,0:T(2,128)(2,1)S(1)} all-gather(bf16[1,2,16]{2,1,0:T(2,128)(2,1)} %bitcast.77), channel_id=1, replica_groups=mesh['dp'=16,'seq'=32] {'dp','seq'}, dimensions={0}, use_global_device_ids=true | all-gather | bytes 32832 | tf_op jit(solution)/shard_map/all_gather | solution.py:89
  1244.9 510.5 %gather_fusion = bf16[147456,16]{1,0:T(8,128)(2,1)} fusion(bf16[16,1280]{0,1:T(8,128)(2,1)S(1)} %maximum_bitcast_fusion, s32[147456]{0:T(1024)S(1)} %broadcast_clamp_fusion), kind=kCustom, calls=%fused_computation | custom fusion | bytes 10027008 | tf_op jit(solution)/shard_map/gather | solution.py:36
  1755.4 30.3 %copy.71 = bf16[9,128,128,16]{2,1,0,3:T(8,128)(2,1)} copy(bf16[9,128,128,16]{3,2,1,0:T(8,128)(2,1)} %bitcast.61) | data formatting | bytes 9437184 | tf_op jit(solution)/shard_map/gather | solution.py:36
  1785.8 150.7 %while.37 = (s32[]{:T(128)}, bf16[128,2048]{1,0:T(8,128)(2,1)S(1)}, bf16[8,128,2048]{1,2,0:T(8,128)(2,1)}, s32[]{:T(128)}) while((s32[]{:T(128)}, bf16[128,2048]{1,0:T(8,128)(2,1)S(1)}, bf16[8,128,2048]{1,2,0:T(8,128)(2,1)}, s32[]{:T(128)}) %tuple.63), condition=%wide.region_3.4_spmd, body=%wide.region_2.3_spmd.sunk | while | flops 2 | bytes 5242985 | solution.py:55
  1785.9 7.8 collective-permute-start.1
  1793.6 11.7 collective-permute-done.1
  1806.5 4.4 collective-permute-start.1
  1810.9 14.7 collective-permute-done.1
  1826.8 1.9 collective-permute-start.1
  1828.8 16.3 collective-permute-done.1
  1846.2 1.9 collective-permute-start.1
  1848.2 16.3 collective-permute-done.1
  1865.6 1.9 collective-permute-start.1
  1867.5 14.7 collective-permute-done.1
  1883.4 1.9 collective-permute-start.1
  1885.3 14.6 collective-permute-done.1
  1901.1 1.9 collective-permute-start.1
  1903.0 14.6 collective-permute-done.1
  1918.8 1.9 collective-permute-start.1
  1920.7 14.7 collective-permute-done.1
  1936.6 5.2 fusion.10
  1942.1 2.3 fusion.17
  1944.8 115.4 %while.36 = (s32[]{:T(128)}, bf16[128,2048]{1,0:T(8,128)(2,1)S(1)}, bf16[8,128,2048]{2,1,0:T(8,128)(2,1)}, s32[]{:T(128)}) while((s32[]{:T(128)}, bf16[128,2048]{1,0:T(8,128)(2,1)S(1)}, bf16[8,128,2048]{2,1,0:T(8,128)(2,1)}, s32[]{:T(128)}) %tuple.66), condition=%wide.region_1.2_spmd, body=%wide.region_0.1_spmd.sunk | while | flops 2 | bytes 4194409 | solution.py:45
  1944.8 1.9 collective-permute-start
  1946.7 12.9 collective-permute-done
  1960.5 1.9 collective-permute-start
  1962.4 14.1 collective-permute-done
  1977.5 1.9 collective-permute-start
  1979.4 9.1 collective-permute-done
  1989.4 4.6 collective-permute-start
  1994.0 6.7 collective-permute-done
  2001.6 7.1 collective-permute-start
  2008.7 6.7 collective-permute-done
  2016.3 7.1 collective-permute-start
  2023.3 6.7 collective-permute-done
  2030.9 7.1 collective-permute-start
  2038.0 6.7 collective-permute-done
  2045.5 7.1 collective-permute-start
  2052.6 6.7 collective-permute-done
  2060.2 4.8 pad_maximum_fusion
  2064.9 5.2 rev.6
  2070.1 6.8 copy.89
  2076.9 5.0 concatenate.35.clone
  2081.9 34.4 %while.38 = (s32[]{:T(128)}, f32[16,1024]{1,0:T(8,128)S(1)}, bf16[16,128,128]{2,1,0:T(8,128)(2,1)S(1)}, bf16[16,1280,128]{1,2,0:T(8,128)(2,1)}, s32[]{:T(128)}, /*index=5*/f32[]{:T(128)}, s32[]{:T(128)}) while((s32[]{:T(128)}, f32[16,1024]{1,0:T(8,128)S(1)}, bf16[16,128,128]{2,1,0:T(8,128)(2,1)S(1)}, bf16[16,1280,128]{1,2,0:T(8,128)(2,1)}, ...), condition=%wide.region_6.7_spmd, body=%wide.region_4.6_spmd.sunk | while | flops 42121984 | bytes 7471721 | solution.py:80
  2117.6 6.4 copy.69
  2124.1 5.4 fusion.6
  2131.0 251.9 %all-reduce.6.cloned.1.call-done = f32[1024,16]{1,0:T(8,128)} async-done(((f32[1024,16]{1,0:T(8,128)}), f32[1024,16]{1,0:T(8,128)}) %all-reduce.6.cloned.1.call-update) | async-done | bytes 65552
  (209 shorter events, 56.6 us)
Async XLA Ops:
  7.2 2375.7 %all-reduce.6.cloned.1.call-start = ((), (), s32[]{:S(2)}) async-start(), calls=%async_computation | async-start | bytes 1048576
  1785.9 19.5 collective-permute-start.1
  1806.5 19.1 collective-permute-start.1
  1826.8 18.2 collective-permute-start.1
  1846.2 18.2 collective-permute-start.1
  1865.6 16.6 collective-permute-start.1
  1883.4 16.5 collective-permute-start.1
  1901.1 16.6 collective-permute-start.1
  1918.8 16.6 collective-permute-start.1
  1936.6 5.6 copy-start.2
  1944.8 14.8 collective-permute-start
  1960.5 16.1 collective-permute-start
  1977.5 11.1 collective-permute-start
  1989.4 11.3 collective-permute-start
  2001.6 13.8 collective-permute-start
  2016.3 13.8 collective-permute-start
  2030.9 13.8 collective-permute-start
  2045.5 13.8 collective-permute-start
  2124.1 5.7 copy-start
  2124.1 5.7 copy-start.1
Sparse Core Ops, SparseCore 0:
  2117.5 265.3 all-reduce.5
where the time goes:
time: 2390 us
  blocking collectives  1230 us (51%)
  local copies, waits for them, and re-layouts  597 us (25%)
  waiting for transfers between devices  439 us (18%)
  starting transfers between devices  62.3 us (3%)
  matrix products  29.8 us (1%)
    all_gather x1, blocking collectives, shards(): all_taps = lax.all_gather(filters, ('dp', 'seq'), axis=0, tiled=True)  1230 us
    gather x2, local copies, waits for them, and re-layouts, build_tiles(): return columns[:, tile_index(lag_blocks, shard_len)]  541 us
    unnamed x2, waiting for transfers between devices  252 us
    ppermute x16, waiting for transfers between devices, shifted(): lax.ppermute(value, axis, [(source, source + steps) for source in range(f...  187 us
    ppermute x16, starting transfers between devices, shifted(): lax.ppermute(value, axis, [(source, source + steps) for source in range(f...  62.3 us
  transfers between devices with their start and end apart: 17, of which 17 were waited for; matrix products, arithmetic and copies ran while one was open for 1% of the time, Pallas kernels for 0%

commit v1 on v0

--- a/solution.py
+++ b/solution.py
@@ -86,7 +86,10 @@
     groups = filters.shape[1]
     group_size = channels // groups
     seq_count = lax.axis_size("seq")
-    all_taps = lax.all_gather(filters, ("dp", "seq"), axis=0, tiled=True)
+    all_taps = jnp.concatenate(
+        lax.all_to_all(jnp.stack([filters] * lax.axis_size(("dp", "seq"))), ("dp", "seq"), 0, 0),
+        axis=0,
+    )
     mixed_in = (pre_gate[0].astype(jnp.float32) * values[0]).astype(jnp.bfloat16)
     gated = (cotangent[0].astype(jnp.float32) * post_gate[0]).astype(jnp.bfloat16)
     history_len = min(-(-K // shard_len), seq_count - 1)

time: 2390 us -> 1240 us (0.52)
  blocking collectives: 1230 us -> 0 us
  waiting for transfers between devices: 439 us -> 503 us
    all_gather x1 -> x0, blocking collectives: 1230 us -> none  [shards(): all_taps = lax.all_gather(filters, ('dp', 'seq'), axis=0, tiled=True)]
    unnamed x2, waiting for transfers between devices: 252 us -> 292 us
  transfers between devices with their start and end apart: 17 -> 18, of which waited for: 17 -> 18; matrix products, arithmetic and copies ran while one was open for 1% -> 1% of each run, Pallas kernels for 0% -> 0%
where the time goes in v1:
time: 1240 us
  local copies, waits for them, and re-layouts  604 us (49%)
  waiting for transfers between devices  503 us (41%)
  starting transfers between devices  73.5 us (6%)
  matrix products  26.4 us (2%)
  between operations  14.2 us (1%)
  other arithmetic  13.6 us (1%)
    gather x2, local copies, waits for them, and re-layouts, build_tiles(): return columns[:, tile_index(lag_blocks, shard_len)]  544 us
    unnamed x2, waiting for transfers between devices  292 us
    ppermute x16, waiting for transfers between devices, shifted(): lax.ppermute(value, axis, [(source, source + steps) for source in range(f...  201 us
    ppermute x16, starting transfers between devices, shifted(): lax.ppermute(value, axis, [(source, source + steps) for source in range(f...  52.6 us
  transfers between devices with their start and end apart: 18, of which 18 were waited for; matrix products, arithmetic and copies ran while one was open for 1% of the time, Pallas kernels for 0%

profile of v1, /device:TPU:24, one launch (start us, length us, event | category | flops | bytes accessed | tf_op | source)
XLA Modules:
  0.0 1237.0 jit_solution(5882294043281908754)
XLA Ops:
  8.7 20.9 %all-to-all-start = ((bf16[512,2,16]{2,1,0:T(2,128)(2,1)}), bf16[512,2,16]{2,1,0:T(2,128)(2,1)S(1)}, u32[]{:S(2)}, u32[]{:S(2)}) async-start(bf16[512,2,16]{2,1,0:T(2,128)(2,1)} %stack.2), calls=%async_computation | async-start | bytes 524288 | tf_op jit(solution)/shard_map/all_to_all | solution.py:90
  34.2 10.2 all-to-all-done
  44.5 514.1 %gather_fusion = bf16[147456,16]{1,0:T(8,128)(2,1)} fusion(bf16[16,1280]{0,1:T(8,128)(2,1)S(1)} %maximum_bitcast_fusion, s32[147456]{0:T(1024)S(1)} %broadcast_clamp_fusion), kind=kCustom, calls=%fused_computation | custom fusion | bytes 10027008 | tf_op jit(solution)/shard_map/gather | solution.py:36
  558.5 30.4 %copy.88 = bf16[9,128,128,16]{2,1,0,3:T(8,128)(2,1)} copy(bf16[9,128,128,16]{3,2,1,0:T(8,128)(2,1)} %bitcast.60) | data formatting | bytes 9437184 | tf_op jit(solution)/shard_map/gather | solution.py:36
  588.9 133.2 %while.37 = (s32[]{:T(128)}, bf16[128,2048]{1,0:T(8,128)(2,1)S(1)}, bf16[8,128,2048]{1,2,0:T(8,128)(2,1)}, s32[]{:T(128)}) while((s32[]{:T(128)}, bf16[128,2048]{1,0:T(8,128)(2,1)S(1)}, bf16[8,128,2048]{1,2,0:T(8,128)(2,1)}, s32[]{:T(128)}) %tuple.76), condition=%wide.region_3.4_spmd, body=%wide.region_2.3_spmd.sunk | while | flops 2 | bytes 5242985 | solution.py:55
  588.9 3.2 collective-permute-start.1
  592.1 15.2 %collective-permute-done.1 = bf16[128,2048]{1,0:T(8,128)(2,1)S(1)} collective-permute-done((bf16[128,2048]{1,0:T(8,128)(2,1)S(1)}, bf16[128,2048]{1,0:T(8,128)(2,1)S(1)}, u32[]{:S(2)}, u32[]{:S(2)}) %collective-permute-start.1) | collective-permute-done | bytes 524320 | tf_op jit(solution)/shard_map/while/body/eval_jaxpr/ppermute | solution.py:13
  608.5 1.9 collective-permute-start.1
  610.4 15.5 %collective-permute-done.1 = bf16[128,2048]{1,0:T(8,128)(2,1)S(1)} collective-permute-done((bf16[128,2048]{1,0:T(8,128)(2,1)S(1)}, bf16[128,2048]{1,0:T(8,128)(2,1)S(1)}, u32[]{:S(2)}, u32[]{:S(2)}) %collective-permute-start.1) | collective-permute-done | bytes 524320 | tf_op jit(solution)/shard_map/while/body/eval_jaxpr/ppermute | solution.py:13
  627.1 1.9 collective-permute-start.1
  629.0 14.5 %collective-permute-done.1 = bf16[128,2048]{1,0:T(8,128)(2,1)S(1)} collective-permute-done((bf16[128,2048]{1,0:T(8,128)(2,1)S(1)}, bf16[128,2048]{1,0:T(8,128)(2,1)S(1)}, u32[]{:S(2)}, u32[]{:S(2)}) %collective-permute-start.1) | collective-permute-done | bytes 524320 | tf_op jit(solution)/shard_map/while/body/eval_jaxpr/ppermute | solution.py:13
  644.7 1.9 collective-permute-start.1
  646.7 13.6 %collective-permute-done.1 = bf16[128,2048]{1,0:T(8,128)(2,1)S(1)} collective-permute-done((bf16[128,2048]{1,0:T(8,128)(2,1)S(1)}, bf16[128,2048]{1,0:T(8,128)(2,1)S(1)}, u32[]{:S(2)}, u32[]{:S(2)}) %collective-permute-start.1) | collective-permute-done | bytes 524320 | tf_op jit(solution)/shard_map/while/body/eval_jaxpr/ppermute | solution.py:13
  661.5 1.9 collective-permute-start.1
  663.4 12.7 %collective-permute-done.1 = bf16[128,2048]{1,0:T(8,128)(2,1)S(1)} collective-permute-done((bf16[128,2048]{1,0:T(8,128)(2,1)S(1)}, bf16[128,2048]{1,0:T(8,128)(2,1)S(1)}, u32[]{:S(2)}, u32[]{:S(2)}) %collective-permute-start.1) | collective-permute-done | bytes 524320 | tf_op jit(solution)/shard_map/while/body/eval_jaxpr/ppermute | solution.py:13
  677.3 1.9 collective-permute-start.1
  679.2 11.8 collective-permute-done.1
  692.3 1.9 collective-permute-start.1
  694.2 11.8 collective-permute-done.1
  707.2 1.9 collective-permute-start.1
  709.1 11.8 collective-permute-done.1
  722.2 5.1 fusion.10
  729.2 137.6 %while.36 = (s32[]{:T(128)}, bf16[128,2048]{1,0:T(8,128)(2,1)S(1)}, bf16[8,128,2048]{2,1,0:T(8,128)(2,1)}, s32[]{:T(128)}) while((s32[]{:T(128)}, bf16[128,2048]{1,0:T(8,128)(2,1)S(1)}, bf16[8,128,2048]{2,1,0:T(8,128)(2,1)}, s32[]{:T(128)}) %tuple.67), condition=%wide.region_1.2_spmd, body=%wide.region_0.1_spmd.sunk | while | flops 2 | bytes 4194409 | solution.py:45
  729.2 1.9 collective-permute-start
  731.2 13.0 %collective-permute-done = bf16[128,2048]{1,0:T(8,128)(2,1)S(1)} collective-permute-done((bf16[128,2048]{1,0:T(8,128)(2,1)S(1)}, bf16[128,2048]{1,0:T(8,128)(2,1)S(1)}, u32[]{:S(2)}, u32[]{:S(2)}) %collective-permute-start) | collective-permute-done | bytes 524320 | tf_op jit(solution)/shard_map/while/body/eval_jaxpr/ppermute | solution.py:13
  745.1 1.9 collective-permute-start
  747.0 14.2 %collective-permute-done = bf16[128,2048]{1,0:T(8,128)(2,1)S(1)} collective-permute-done((bf16[128,2048]{1,0:T(8,128)(2,1)S(1)}, bf16[128,2048]{1,0:T(8,128)(2,1)S(1)}, u32[]{:S(2)}, u32[]{:S(2)}) %collective-permute-start) | collective-permute-done | bytes 524320 | tf_op jit(solution)/shard_map/while/body/eval_jaxpr/ppermute | solution.py:13
  762.1 1.9 collective-permute-start
  764.0 14.2 %collective-permute-done = bf16[128,2048]{1,0:T(8,128)(2,1)S(1)} collective-permute-done((bf16[128,2048]{1,0:T(8,128)(2,1)S(1)}, bf16[128,2048]{1,0:T(8,128)(2,1)S(1)}, u32[]{:S(2)}, u32[]{:S(2)}) %collective-permute-start) | collective-permute-done | bytes 524320 | tf_op jit(solution)/shard_map/while/body/eval_jaxpr/ppermute | solution.py:13
  779.2 3.0 collective-permute-start
  782.1 12.4 collective-permute-done
  795.4 6.0 collective-permute-start
  801.4 12.2 collective-permute-done
  814.4 7.1 collective-permute-start
  821.5 11.3 collective-permute-done
  833.7 7.1 collective-permute-start
  840.8 10.4 collective-permute-done
  852.1 7.1 collective-permute-start
  859.2 6.7 collective-permute-done
  866.8 6.5 copy.86
  873.3 5.1 pad_maximum_fusion
  879.7 1.8 fusion.6
  881.9 5.2 rev.6
  887.1 6.7 copy.106
  893.8 5.0 concatenate.35.clone
  898.8 34.7 %while.38 = (s32[]{:T(128)}, f32[16,1024]{1,0:T(8,128)S(1)}, bf16[16,128,128]{2,1,0:T(8,128)(2,1)}, bf16[16,1280,128]{1,2,0:T(8,128)(2,1)}, s32[]{:T(128)}, /*index=5*/f32[]{:T(128)}, s32[]{:T(128)}) while((s32[]{:T(128)}, f32[16,1024]{1,0:T(8,128)S(1)}, bf16[16,128,128]{2,1,0:T(8,128)(2,1)}, bf16[16,1280,128]{1,2,0:T(8,128)(2,1)}, s32[]{:T(128)}, ...), condition=%wide.region_6.7_spmd, body=%wide.region_4.6_spmd.sunk | while | flops 42121984 | bytes 7471721 | solution.py:80
  934.6 2.5 fusion.21
  937.1 291.9 %all-reduce.6.cloned.1.call-done = f32[1024,16]{1,0:T(8,128)} async-done(((f32[1024,16]{1,0:T(8,128)}), f32[1024,16]{1,0:T(8,128)}) %all-reduce.6.cloned.1.call-update) | async-done | bytes 65552
  (217 shorter events, 62.0 us)
Async XLA Ops:
  8.7 35.7 %all-to-all-start = ((bf16[512,2,16]{2,1,0:T(2,128)(2,1)}), bf16[512,2,16]{2,1,0:T(2,128)(2,1)S(1)}, u32[]{:S(2)}, u32[]{:S(2)}) async-start(bf16[512,2,16]{2,1,0:T(2,128)(2,1)} %stack.2), calls=%async_computation | async-start | bytes 524288 | tf_op jit(solution)/shard_map/all_to_all | solution.py:90
  29.6 1199.3 %all-reduce.6.cloned.1.call-start = ((), (), s32[]{:S(2)}) async-start(), calls=%async_computation.1 | async-start | bytes 1048576
  588.9 133.2 %copy-start.3 = (bf16[1,128,2048]{1,2,0:T(8,128)(2,1)S(1)}, bf16[1,128,2048]{1,2,0:T(8,128)(2,1)}, u32[]{:S(2)}) copy-start(bf16[1,128,2048]{1,2,0:T(8,128)(2,1)} %copy.90) | copy-start | bytes 1572868
  588.9 18.4 %collective-permute-start.1 = (bf16[128,2048]{1,0:T(8,128)(2,1)S(1)}, bf16[128,2048]{1,0:T(8,128)(2,1)S(1)}, u32[]{:S(2)}, u32[]{:S(2)}) collective-permute-start(bf16[128,2048]{1,0:T(8,128)(2,1)S(1)} %get-tuple-element.208), channel_id=1, source_target_pairs={{1,0},{2,1},{3,2},{4,3},{5,4},{6,5},{7,6},{8,7},{9,8},{10,9},{11,1... | collective-permute-start | bytes 1572872 | tf_op jit(solution)/shard_map/while/body/eval_jaxpr/ppermute | solution.py:13
  608.5 17.4 %collective-permute-start.1 = (bf16[128,2048]{1,0:T(8,128)(2,1)S(1)}, bf16[128,2048]{1,0:T(8,128)(2,1)S(1)}, u32[]{:S(2)}, u32[]{:S(2)}) collective-permute-start(bf16[128,2048]{1,0:T(8,128)(2,1)S(1)} %get-tuple-element.208), channel_id=1, source_target_pairs={{1,0},{2,1},{3,2},{4,3},{5,4},{6,5},{7,6},{8,7},{9,8},{10,9},{11,1... | collective-permute-start | bytes 1572872 | tf_op jit(solution)/shard_map/while/body/eval_jaxpr/ppermute | solution.py:13
  627.1 16.5 %collective-permute-start.1 = (bf16[128,2048]{1,0:T(8,128)(2,1)S(1)}, bf16[128,2048]{1,0:T(8,128)(2,1)S(1)}, u32[]{:S(2)}, u32[]{:S(2)}) collective-permute-start(bf16[128,2048]{1,0:T(8,128)(2,1)S(1)} %get-tuple-element.208), channel_id=1, source_target_pairs={{1,0},{2,1},{3,2},{4,3},{5,4},{6,5},{7,6},{8,7},{9,8},{10,9},{11,1... | collective-permute-start | bytes 1572872 | tf_op jit(solution)/shard_map/while/body/eval_jaxpr/ppermute | solution.py:13
  644.7 15.6 %collective-permute-start.1 = (bf16[128,2048]{1,0:T(8,128)(2,1)S(1)}, bf16[128,2048]{1,0:T(8,128)(2,1)S(1)}, u32[]{:S(2)}, u32[]{:S(2)}) collective-permute-start(bf16[128,2048]{1,0:T(8,128)(2,1)S(1)} %get-tuple-element.208), channel_id=1, source_target_pairs={{1,0},{2,1},{3,2},{4,3},{5,4},{6,5},{7,6},{8,7},{9,8},{10,9},{11,1... | collective-permute-start | bytes 1572872 | tf_op jit(solution)/shard_map/while/body/eval_jaxpr/ppermute | solution.py:13
  661.5 14.6 %collective-permute-start.1 = (bf16[128,2048]{1,0:T(8,128)(2,1)S(1)}, bf16[128,2048]{1,0:T(8,128)(2,1)S(1)}, u32[]{:S(2)}, u32[]{:S(2)}) collective-permute-start(bf16[128,2048]{1,0:T(8,128)(2,1)S(1)} %get-tuple-element.208), channel_id=1, source_target_pairs={{1,0},{2,1},{3,2},{4,3},{5,4},{6,5},{7,6},{8,7},{9,8},{10,9},{11,1... | collective-permute-start | bytes 1572872 | tf_op jit(solution)/shard_map/while/body/eval_jaxpr/ppermute | solution.py:13
  677.3 13.8 %collective-permute-start.1 = (bf16[128,2048]{1,0:T(8,128)(2,1)S(1)}, bf16[128,2048]{1,0:T(8,128)(2,1)S(1)}, u32[]{:S(2)}, u32[]{:S(2)}) collective-permute-start(bf16[128,2048]{1,0:T(8,128)(2,1)S(1)} %get-tuple-element.208), channel_id=1, source_target_pairs={{1,0},{2,1},{3,2},{4,3},{5,4},{6,5},{7,6},{8,7},{9,8},{10,9},{11,1... | collective-permute-start | bytes 1572872 | tf_op jit(solution)/shard_map/while/body/eval_jaxpr/ppermute | solution.py:13
  692.3 13.8 %collective-permute-start.1 = (bf16[128,2048]{1,0:T(8,128)(2,1)S(1)}, bf16[128,2048]{1,0:T(8,128)(2,1)S(1)}, u32[]{:S(2)}, u32[]{:S(2)}) collective-permute-start(bf16[128,2048]{1,0:T(8,128)(2,1)S(1)} %get-tuple-element.208), channel_id=1, source_target_pairs={{1,0},{2,1},{3,2},{4,3},{5,4},{6,5},{7,6},{8,7},{9,8},{10,9},{11,1... | collective-permute-start | bytes 1572872 | tf_op jit(solution)/shard_map/while/body/eval_jaxpr/ppermute | solution.py:13
  707.2 13.8 %collective-permute-start.1 = (bf16[128,2048]{1,0:T(8,128)(2,1)S(1)}, bf16[128,2048]{1,0:T(8,128)(2,1)S(1)}, u32[]{:S(2)}, u32[]{:S(2)}) collective-permute-start(bf16[128,2048]{1,0:T(8,128)(2,1)S(1)} %get-tuple-element.208), channel_id=1, source_target_pairs={{1,0},{2,1},{3,2},{4,3},{5,4},{6,5},{7,6},{8,7},{9,8},{10,9},{11,1... | collective-permute-start | bytes 1572872 | tf_op jit(solution)/shard_map/while/body/eval_jaxpr/ppermute | solution.py:13
  722.1 5.4 copy-start.1
  722.2 5.4 copy-start.2
  729.2 14.9 %collective-permute-start = (bf16[128,2048]{1,0:T(8,128)(2,1)S(1)}, bf16[128,2048]{1,0:T(8,128)(2,1)S(1)}, u32[]{:S(2)}, u32[]{:S(2)}) collective-permute-start(bf16[128,2048]{1,0:T(8,128)(2,1)S(1)} %get-tuple-element.220), channel_id=1, source_target_pairs={{0,1},{1,2},{2,3},{3,4},{4,5},{5,6},{6,7},{7,8},{8,9},{9,10},{10,1... | collective-permute-start | bytes 1572872 | tf_op jit(solution)/shard_map/while/body/eval_jaxpr/ppermute | solution.py:13
  745.1 16.1 %collective-permute-start = (bf16[128,2048]{1,0:T(8,128)(2,1)S(1)}, bf16[128,2048]{1,0:T(8,128)(2,1)S(1)}, u32[]{:S(2)}, u32[]{:S(2)}) collective-permute-start(bf16[128,2048]{1,0:T(8,128)(2,1)S(1)} %get-tuple-element.220), channel_id=1, source_target_pairs={{0,1},{1,2},{2,3},{3,4},{4,5},{5,6},{6,7},{7,8},{8,9},{9,10},{10,1... | collective-permute-start | bytes 1572872 | tf_op jit(solution)/shard_map/while/body/eval_jaxpr/ppermute | solution.py:13
  762.1 16.1 %collective-permute-start = (bf16[128,2048]{1,0:T(8,128)(2,1)S(1)}, bf16[128,2048]{1,0:T(8,128)(2,1)S(1)}, u32[]{:S(2)}, u32[]{:S(2)}) collective-permute-start(bf16[128,2048]{1,0:T(8,128)(2,1)S(1)} %get-tuple-element.220), channel_id=1, source_target_pairs={{0,1},{1,2},{2,3},{3,4},{4,5},{5,6},{6,7},{7,8},{8,9},{9,10},{10,1... | collective-permute-start | bytes 1572872 | tf_op jit(solution)/shard_map/while/body/eval_jaxpr/ppermute | solution.py:13
  779.2 15.3 %collective-permute-start = (bf16[128,2048]{1,0:T(8,128)(2,1)S(1)}, bf16[128,2048]{1,0:T(8,128)(2,1)S(1)}, u32[]{:S(2)}, u32[]{:S(2)}) collective-permute-start(bf16[128,2048]{1,0:T(8,128)(2,1)S(1)} %get-tuple-element.220), channel_id=1, source_target_pairs={{0,1},{1,2},{2,3},{3,4},{4,5},{5,6},{6,7},{7,8},{8,9},{9,10},{10,1... | collective-permute-start | bytes 1572872 | tf_op jit(solution)/shard_map/while/body/eval_jaxpr/ppermute | solution.py:13
  795.4 18.2 %collective-permute-start = (bf16[128,2048]{1,0:T(8,128)(2,1)S(1)}, bf16[128,2048]{1,0:T(8,128)(2,1)S(1)}, u32[]{:S(2)}, u32[]{:S(2)}) collective-permute-start(bf16[128,2048]{1,0:T(8,128)(2,1)S(1)} %get-tuple-element.220), channel_id=1, source_target_pairs={{0,1},{1,2},{2,3},{3,4},{4,5},{5,6},{6,7},{7,8},{8,9},{9,10},{10,1... | collective-permute-start | bytes 1572872 | tf_op jit(solution)/shard_map/while/body/eval_jaxpr/ppermute | solution.py:13
  814.4 18.4 %collective-permute-start = (bf16[128,2048]{1,0:T(8,128)(2,1)S(1)}, bf16[128,2048]{1,0:T(8,128)(2,1)S(1)}, u32[]{:S(2)}, u32[]{:S(2)}) collective-permute-start(bf16[128,2048]{1,0:T(8,128)(2,1)S(1)} %get-tuple-element.220), channel_id=1, source_target_pairs={{0,1},{1,2},{2,3},{3,4},{4,5},{5,6},{6,7},{7,8},{8,9},{9,10},{10,1... | collective-permute-start | bytes 1572872 | tf_op jit(solution)/shard_map/while/body/eval_jaxpr/ppermute | solution.py:13
  833.7 17.5 %collective-permute-start = (bf16[128,2048]{1,0:T(8,128)(2,1)S(1)}, bf16[128,2048]{1,0:T(8,128)(2,1)S(1)}, u32[]{:S(2)}, u32[]{:S(2)}) collective-permute-start(bf16[128,2048]{1,0:T(8,128)(2,1)S(1)} %get-tuple-element.220), channel_id=1, source_target_pairs={{0,1},{1,2},{2,3},{3,4},{4,5},{5,6},{6,7},{7,8},{8,9},{9,10},{10,1... | collective-permute-start | bytes 1572872 | tf_op jit(solution)/shard_map/while/body/eval_jaxpr/ppermute | solution.py:13
  852.1 13.8 %collective-permute-start = (bf16[128,2048]{1,0:T(8,128)(2,1)S(1)}, bf16[128,2048]{1,0:T(8,128)(2,1)S(1)}, u32[]{:S(2)}, u32[]{:S(2)}) collective-permute-start(bf16[128,2048]{1,0:T(8,128)(2,1)S(1)} %get-tuple-element.220), channel_id=1, source_target_pairs={{0,1},{1,2},{2,3},{3,4},{4,5},{5,6},{6,7},{7,8},{8,9},{9,10},{10,1... | collective-permute-start | bytes 1572872 | tf_op jit(solution)/shard_map/while/body/eval_jaxpr/ppermute | solution.py:13
  866.8 11.7 slice-start
  873.3 5.2 slice-start.1
  873.3 6.4 copy-start
Sparse Core Ops, SparseCore 0:
  934.7 294.1 all-reduce.5
